TPU v7x, 32 devices: a whole 2x2x4 slice. The times are simulated.
32 devices in a mesh: req: 2 (over x), ctx: 4 (over y, core), tp: 4 (over z).
Axes of the slice: x: 2, y: 2, z: 4, core: 2. Of those that a mesh axis runs over, the one named last changes fastest.
Arguments:
- queries: bfloat16 [512, 16, 128], P('req', 'tp'), may hold values from -5 to 5
- new_keys: bfloat16 [512, 4, 128], P('req', 'tp'), may hold values from -5 to 5
- new_values: bfloat16 [512, 4, 128], P('req', 'tp'), may hold values from -24 to 24
- cache_keys: bfloat16 [2, 8192, 4, 128], P('req', 'ctx', 'tp'), may hold values from -5 to 5
- cache_values: bfloat16 [2, 8192, 4, 128], P('req', 'ctx', 'tp'), may hold values from -24 to 24
- cache_lengths: int32 [2], replicated, may hold values from 1 to 8192, as said below
- residual: bfloat16 [512, 2048], P(('req', 'ctx'), 'tp'), may hold values from -24 to 24
- out_weight: bfloat16 [2048, 2048], P('tp', 'ctx'), may hold values from -0.52734375 to 0.52734375
- norm_gain: float32 [2048], replicated, may hold values from 0.1 to 1.9
- expert_ids: int32 [512, 6], P(('req', 'ctx')), may hold values from 0 to 63, all different within a row; in each aligned block of 64 rows (0 to 63, 64 to 127, ...) at most 8 rows name the same one
- gate_weights: float32 [512, 6], P(('req', 'ctx')), may hold values from 0.1 to 1
- w_gate: bfloat16 [64, 2048, 1408], P('req', 'ctx', 'tp'), may hold values from -0.125 to 0.125
- w_up: bfloat16 [64, 2048, 1408], P('req', 'ctx', 'tp'), may hold values from -0.125 to 0.125
- w_down: bfloat16 [64, 1408, 2048], P('req', 'tp', 'ctx'), may hold values from -0.15625 to 0.15625
Outputs:
- layer_out: bfloat16 [512, 2048], P(('req', 'ctx'), 'tp')
Inputs may be any that keep to these rules, and one draw needn't show every extreme that they name: `cache_lengths`: the longest cached length equals 8192. `expert_ids`: within each aligned block of 64 tokens no expert is named by more than 8 routes, a bound that some block reaches.
All inputs are finite; a program needn't handle non-finite values.
Results may differ from a plain program's by a relative error of at most 0.006.
Values may be sent and summed in bfloat16 or wider, within the bound.
A program may use at most 384 MiB of HBM per device.

v0:
```python
import jax
import jax.numpy as jnp
from jax import lax
from jax.sharding import PartitionSpec as P

TOP = 6
CAP = 8
MASKED = -1e30


def attention_part(queries, new_keys, new_values, cache_keys, cache_values, length):
    ctx_pos, ctx_count = (lax.axis_index("ctx"), lax.axis_size("ctx"))
    tok_dev, heads, hd = queries.shape
    cache_dev = cache_keys.shape[1]
    block = tok_dev // ctx_count
    rows = heads * block
    q = queries.reshape(ctx_count, block, heads, hd).transpose(0, 2, 1, 3)
    q = q.reshape(ctx_count * rows, hd)
    keys = jnp.concatenate([cache_keys[0, :, 0, :], new_keys[:, 0, :]], 0)
    values = jnp.concatenate([cache_values[0, :, 0, :], new_values[:, 0, :]], 0)
    scores = jnp.dot(keys, q.T, preferred_element_type=jnp.float32) * hd ** (-0.5)
    key_at = jnp.arange(cache_dev + tok_dev, dtype=jnp.int32)[:, None]
    row_at = jnp.arange(ctx_count * rows, dtype=jnp.int32)[None, :]
    token = row_at // rows * block + row_at % block
    valid = jnp.where(
        key_at < cache_dev,
        ctx_pos * cache_dev + key_at < length,
        jnp.logical_and(ctx_pos == ctx_count - 1, key_at - cache_dev <= token),
    )
    scores = jnp.where(valid, scores, MASKED)
    top = jnp.max(scores, 0, keepdims=True)
    weights = jnp.where(valid, jnp.exp(scores - top), 0.0)
    total = jnp.sum(weights, 0, keepdims=True)
    sums = lax.dot_general(
        values,
        weights.astype(jnp.bfloat16),
        (((0,), (0,)), ((), ())),
        preferred_element_type=jnp.float32,
    )
    pack = jnp.concatenate([sums, top, total, jnp.zeros((6, ctx_count * rows), jnp.float32)], 0)
    return pack.reshape(hd + 8, ctx_count, rows).transpose(1, 0, 2)


def merge(packs, hd, heads):
    top = jnp.max(packs[:, hd : hd + 1], 0)
    factor = jnp.exp(packs[:, hd : hd + 1] - top)
    total = jnp.sum(factor * packs[:, hd + 1 : hd + 2], 0)
    out = (jnp.sum(factor * packs[:, :hd], 0) / total).astype(jnp.bfloat16)
    block = out.shape[1] // heads
    return out.reshape(hd, heads, block).transpose(2, 1, 0).reshape(block, heads * hd)


def route_tables(expert_ids, gate_weights, exp_dev):
    block = expert_ids.shape[0]
    both = jnp.concatenate([expert_ids.astype(jnp.float32), gate_weights], 1)
    both = lax.all_gather(both, ("req", "ctx"))
    blocks = both.shape[0]
    ids = both[:, :, :TOP].astype(jnp.int32)
    gates = both[:, :, TOP:]
    first = lax.axis_index("req") * exp_dev
    experts = first + jnp.arange(exp_dev, dtype=jnp.int32)
    hits = ids[:, :, :, None] == experts
    gate_at = jnp.sum(jnp.where(hits, gates[..., None], 0.0), 2)
    hit = jnp.any(hits, 2)
    earlier = jnp.tril(jnp.ones((block, block), jnp.bfloat16), -1)
    rank = jnp.einsum(
        "ij,bje->bie", earlier, hit.astype(jnp.bfloat16), preferred_element_type=jnp.float32
    )
    code = jnp.arange(blocks, dtype=jnp.int32)[:, None, None] * CAP + rank.astype(jnp.int32)
    code = jnp.where(hit, code, -1)
    flat = (blocks * block, exp_dev)
    return (code.reshape(flat).T, gate_at.reshape(flat).T)


def body(
    queries,
    new_keys,
    new_values,
    cache_keys,
    cache_values,
    cache_lengths,
    residual,
    out_weight,
    norm_gain,
    expert_ids,
    gate_weights,
    w_gate,
    w_up,
    w_down,
):
    ctx_pos, tp_pos, req_pos = (lax.axis_index(a) for a in ("ctx", "tp", "req"))
    ctx_count, req_count = (lax.axis_size("ctx"), lax.axis_size("req"))
    tok_dev, heads, hd = queries.shape
    block, share = residual.shape
    exp_dev = w_gate.shape[0]
    slots = req_count * ctx_count * CAP
    length = lax.dynamic_index_in_dim(cache_lengths, req_pos, 0, keepdims=False)
    code, gate_at = route_tables(expert_ids, gate_weights, exp_dev)
    swap = [
        (a * ctx_count + b, b * ctx_count + a) for a in range(ctx_count) for b in range(ctx_count)
    ]
    residual_t = lax.ppermute(residual, ("ctx", "tp"), swap)
    packs = attention_part(queries, new_keys, new_values, cache_keys, cache_values, length)
    packs = lax.all_to_all(packs, "ctx", 0, 0, tiled=True)
    attended = merge(packs, hd, heads)
    attended = lax.all_gather(attended, "ctx", tiled=True)
    part = jnp.dot(attended, out_weight, preferred_element_type=jnp.float32)
    part = part.reshape(-1, block, share)
    part = lax.all_to_all(part, "tp", 0, 0, tiled=True)
    hidden = jnp.sum(part, 0) + residual_t.astype(jnp.float32)
    squares = jnp.sum(hidden * hidden, 1)
    gain = lax.dynamic_slice_in_dim(norm_gain, ctx_pos * share, share, 0)
    scaled = (hidden * gain).astype(jnp.bfloat16)
    squares = lax.psum(squares, "ctx")
    factor = lax.rsqrt(squares / norm_gain.shape[0] + 1e-06)
    factor = lax.all_gather(factor, ("req", "tp"), tiled=True)
    scaled = lax.all_gather(scaled, ("req", "tp"), tiled=True)
    pick = code[:, None, :] == jnp.arange(slots, dtype=jnp.int32)[None, :, None]
    row_factor = jnp.sum(jnp.where(pick, factor, 0.0), -1, keepdims=True)
    row_gate = jnp.sum(jnp.where(pick, gate_at[:, None, :], 0.0), -1, keepdims=True)
    pick = pick.astype(jnp.bfloat16)
    rows = jnp.einsum("est,td->esd", pick, scaled, preferred_element_type=jnp.bfloat16)
    gate = jnp.einsum("esd,edf->esf", rows, w_gate, preferred_element_type=jnp.float32)
    up = jnp.einsum("esd,edf->esf", rows, w_up, preferred_element_type=jnp.float32)
    both = jnp.stack([gate, up], 2).astype(jnp.bfloat16)
    both = both.reshape(ctx_count, exp_dev * slots // ctx_count, 2, -1)
    both = lax.all_to_all(both, "ctx", 0, 0, tiled=True)
    both = both.astype(jnp.float32).sum(0)
    per = exp_dev * slots // ctx_count
    mine = lax.dynamic_slice_in_dim(row_factor.reshape(-1, 1), ctx_pos * per, per, 0)
    inner = (jax.nn.silu(both[:, 0] * mine) * (both[:, 1] * mine)).astype(jnp.bfloat16)
    inner = lax.all_gather(inner, "ctx", tiled=True).reshape(exp_dev, slots, -1)
    down = jnp.einsum("esf,efd->esd", inner, w_down, preferred_element_type=jnp.float32)
    down = (down * row_gate).astype(jnp.bfloat16)
    mixed = jnp.einsum("est,esd->td", pick, down, preferred_element_type=jnp.float32)
    mixed = mixed.astype(jnp.bfloat16).reshape(-1, block, share)
    mixed = lax.all_to_all(mixed, ("req", "tp"), 0, 0, tiled=True)
    out = hidden + jnp.sum(mixed.astype(jnp.float32), 0)
    return lax.ppermute(out.astype(jnp.bfloat16), ("ctx", "tp"), swap)


def solution(mesh):
    in_specs = (
        P("req", "tp", None),
        P("req", "tp", None),
        P("req", "tp", None),
        P("req", "ctx", "tp", None),
        P("req", "ctx", "tp", None),
        P(),
        P(("req", "ctx"), "tp"),
        P("tp", "ctx"),
        P(),
        P(("req", "ctx"), None),
        P(("req", "ctx"), None),
        P("req", "ctx", "tp"),
        P("req", "ctx", "tp"),
        P("req", "tp", "ctx"),
    )
    out_specs = P(("req", "ctx"), "tp")
    return jax.shard_map(body, mesh=mesh, in_specs=in_specs, out_specs=out_specs, check_vma=False)
```

profile of v0, /device:TPU:4, one launch (start us, length us, event | category | flops | bytes accessed | tf_op | source)
XLA Modules:
  0.0 254.7 jit_solution(7631431469196999747)
XLA Ops:
  6.6 1.0 copy.55
  7.6 1.2 dynamic_slice.10
  8.9 0.7 add_compare_fusion
  9.5 6.5 %fusion = (f32[1024]{0:T(1024)S(1)}, f32[2304,1024]{1,0:T(8,128)S(1)}) fusion(s32[1024]{0:T(1024)S(1)} %fusion.38, s32[2304]{0:T(1024)S(1)} %iota_add_fusion, pred[2304]{0:T(1024)(128)(4,1)S(1)} %get-tuple-element.17, pred[2304]{0:T(1024)(128)(4,1)S(1)} %get-tuple-element.18, pred[]{:T(512)S(6)} %eq.16, bf16[1024,128]{1,0:T(8,128)(2,1)S(1)} %bitcast.83, ...), kind=kOutput, calls=%fused_computation.3 | convolution fusion | flops 619314176 | bytes 10311169 | tf_op jit(solution)/shard_map/dot_general | solution.py:21
  16.0 4.7 %fusion.1 = f32[1024]{0:T(1024)S(1)} fusion(f32[2304,1024]{1,0:T(8,128)S(1)} %get-tuple-element.16, f32[1024]{0:T(1024)S(1)} %get-tuple-element.15, s32[1024]{0:T(1024)S(1)} %fusion.38, s32[2304]{0:T(1024)S(1)} %iota_add_fusion, pred[2304]{0:T(1024)(128)(4,1)S(1)} %get-tuple-element.17, pred[2304]{0:T(1024)(128)(4,1)S(1)} %get-tuple-element.18, pred[]{:T(512)S(6)} %eq.16), kind=kLoop, calls=%fused_computation.5 | loop fusion | flops 18873344 | bytes 9463297 | tf_op jit(solution)/shard_map/reduce_sum | solution.py:33
  20.8 4.0 %fusion.3 = f32[128,1024]{1,0:T(8,128)S(1)} fusion(f32[2304,1024]{1,0:T(8,128)S(1)} %get-tuple-element.16, f32[1024]{0:T(1024)S(1)} %get-tuple-element.15, s32[1024]{0:T(1024)S(1)} %fusion.38, s32[2304]{0:T(1024)S(1)} %iota_add_fusion, pred[2304]{0:T(1024)(128)(4,1)S(1)} %get-tuple-element.17, pred[2304]{0:T(1024)(128)(4,1)S(1)} %get-tuple-element.18, ...), kind=kOutput, calls=%fused_computation.7 | convolution fusion | flops 624033792 | bytes 10573313 | tf_op jit(solution)/shard_map/dot_general | solution.py:34
  25.0 0.9 maximum_bitcast_fusion
  25.9 3.5 %all-to-all-start = ((f32[4,136,256]{2,1,0:T(8,128)}), f32[4,136,256]{2,1,0:T(8,128)S(1)}, u32[]{:S(2)}, u32[]{:S(2)}) async-start(f32[4,136,256]{2,1,0:T(8,128)} %maximum_bitcast_fusion), calls=%async_computation | async-start | bytes 1114112 | tf_op jit(solution)/shard_map/all_to_all | solution.py:104
  29.4 4.4 %collective-permute-start = (bf16[64,512]{1,0:T(8,128)(2,1)S(1)}, bf16[64,512]{1,0:T(8,128)(2,1)S(1)}, u32[]{:S(2)}, u32[]{:S(2)}) collective-permute-start(bf16[64,512]{1,0:T(8,128)(2,1)S(1)} %copy-done.14), channel_id=1, source_target_pairs={{0,0},{1,4},{2,8},{3,12},{4,1},{5,5},{6,9},{7,13},{8,2},{9,6},{10,... | collective-permute-start | bytes 196616 | tf_op jit(solution)/shard_map/ppermute | solution.py:102
  33.9 9.2 %all-gather.1 = f32[8,64,12]{1,2,0:T(8,128)S(1)} all-gather(f32[1,64,12]{1,2,0:T(8,128)S(1)} %maximum_bitcast_fusion.1), channel_id=2, replica_groups=mesh['req'=2,'ctx'=4,'tp'=4] {'req','ctx'}, dimensions={0}, use_global_device_ids=true | all-gather | bytes 27648 | tf_op jit(solution)/shard_map/all_gather | solution.py:56
  43.5 5.8 %all_gather.18 = bf16[256,512]{1,0:T(8,128)(2,1)S(1)} all-gather(bf16[64,512]{1,0:T(8,128)(2,1)S(1)} %copy_bitcast_fusion.1), channel_id=1, replica_groups=mesh['req'=2,'ctx'=4,'tp'=4] {'ctx'}, dimensions={0}, use_global_device_ids=true | all-gather | bytes 327680 | tf_op jit(solution)/shard_map/all_gather | solution.py:106
  49.4 1.1 fusion.53
  50.5 5.1 %all-to-all-start.1 = ((f32[4,64,512]{2,1,0:T(8,128)}), f32[4,64,512]{2,1,0:T(8,128)S(1)}, u32[]{:S(2)}, u32[]{:S(2)}) async-start(f32[4,64,512]{2,1,0:T(8,128)} %bitcast.13), calls=%async_computation.1 | async-start | bytes 1048576 | tf_op jit(solution)/shard_map/all_to_all | solution.py:109
  57.4 0.8 dynamic_slice.11
  58.2 12.4 %all-to-all-done.1 = f32[4,64,512]{2,1,0:T(8,128)S(1)} async-done(((f32[4,64,512]{2,1,0:T(8,128)}), f32[4,64,512]{2,1,0:T(8,128)S(1)}, u32[]{:S(2)}, u32[]{:S(2)}) %all-to-all-start.1) | async-done | bytes 524320 | tf_op jit(solution)/shard_map/all_to_all | solution.py:109
  70.8 32.5 %all_gather.21 = bf16[512,512]{1,0:T(8,128)(2,1)S(1)} all-gather(bf16[64,512]{1,0:T(8,128)(2,1)S(1)} %get-tuple-element.12), channel_id=1, replica_groups=mesh['req'=2,'ctx'=4,'tp'=4] {'req','tp'}, dimensions={0}, use_global_device_ids=true | all-gather | bytes 589824 | tf_op jit(solution)/shard_map/all_gather | solution.py:117
  103.3 1.3 fusion.6
  104.6 8.6 %convolution_convert_fusion = bf16[32,64,352]{2,1,0:T(8,128)(2,1)} fusion(bf16[32,64,512]{2,1,0:T(8,128)(2,1)S(1)} %fusion.6, bf16[32,512,352]{1,2,0:T(8,128)(2,1)} %param.26), kind=kOutput, calls=%fused_computation.17 | convolution fusion | flops 738918400 | bytes 15073280 | tf_op jit(solution)/shard_map/esd,edf->esf/dot_general | solution.py:124
  113.2 2.5 copy.63
  115.7 8.6 %convolution_convert_fusion.1 = bf16[32,64,352]{2,1,0:T(8,128)(2,1)} fusion(bf16[32,64,512]{2,1,0:T(8,128)(2,1)S(1)} %fusion.6, bf16[32,512,352]{1,2,0:T(8,128)(2,1)} %param.25), kind=kOutput, calls=%fused_computation.18 | convolution fusion | flops 738918400 | bytes 15073280 | tf_op jit(solution)/shard_map/esd,edf->esf/dot_general | solution.py:123
  124.3 1.7 copy.62
  126.0 3.2 %pad_maximum_fusion = bf16[4,512,2,352]{1,3,2,0:T(8,128)(2,1)} fusion(bf16[4,512,1,352]{1,3,2,0:T(8,128)(2,1)} %copy.63, bf16[4,512,1,352]{1,3,2,0:T(8,128)(2,1)S(1)} %copy.62), kind=kLoop, calls=%fused_computation.14 | loop fusion | flops 1441792 | bytes 5767168 | tf_op jit(solution)/shard_map/stack | solution.py:125
  129.3 5.4 %all-to-all-start.2 = ((bf16[4,512,2,352]{1,3,2,0:T(8,128)(2,1)}), bf16[4,512,2,352]{1,3,2,0:T(8,128)(2,1)S(1)}, u32[]{:S(2)}, u32[]{:S(2)}) async-start(bf16[4,512,2,352]{1,3,2,0:T(8,128)(2,1)} %pad_maximum_fusion), calls=%async_computation.2 | async-start | bytes 5767168 | tf_op jit(solution)/shard_map/all_to_all | solution.py:127
  136.3 33.5 %psum.7 = f32[64]{0:T(128)S(1)} all-reduce(f32[64]{0:T(128)S(1)} %get-tuple-element.11), channel_id=1, replica_groups=mesh['req'=2,'ctx'=4,'tp'=4] {'ctx'}, use_global_device_ids=true, to_apply=%region_9.10 | all-reduce | flops 64 | bytes 512 | tf_op jit(solution)/shard_map/psum | solution.py:114
  169.9 18.9 %all-reduce = f32[512]{0:T(512)S(1)} all-reduce(f32[512]{0:T(512)S(1)} %rsqrt_dynamic-update-slice_fusion), channel_id=1, replica_groups=mesh['req'=2,'ctx'=4,'tp'=4] {'req','tp'}, use_global_device_ids=true, to_apply=%add | all-reduce | flops 512 | bytes 4096
  188.8 1.5 select_reduce_fusion
  191.5 1.0 fusion.16
  192.5 17.0 %all-gather.4.cloned.1.call-done = bf16[2048,352]{1,0:T(8,128)(2,1)} async-done(((bf16[512,352]{1,0:T(8,128)(2,1)}), bf16[2048,352]{1,0:T(8,128)(2,1)}) %all-gather.4.cloned.1.call-update) | async-done | bytes 1441808 | tf_op jit(solution)/shard_map/all_gather | solution.py:132
  209.5 8.2 %fusion.10 = bf16[512,512]{1,0:T(8,128)(2,1)S(1)} fusion(s32[32,512]{1,0:T(8,128)S(1)} %bitcast.86, bf16[32,64,352]{2,1,0:T(8,128)(2,1)} %bitcast.92, bf16[32,352,512]{2,1,0:T(8,128)(2,1)} %param.27, f32[32,64]{1,0:T(8,128)S(1)} %get-tuple-element.5), kind=kOutput, calls=%fused_computation.20 | convolution fusion | flops 1815347200 | bytes 13574144 | tf_op jit(solution)/shard_map/est,esd->td/dot_general | solution.py:135
  217.8 21.4 %all_to_all.20 = bf16[8,64,512]{2,1,0:T(8,128)(2,1)S(1)} all-to-all(bf16[8,64,512]{2,1,0:T(8,128)(2,1)S(1)} %bitcast.81), channel_id=1, replica_groups=mesh['req'=2,'ctx'=4,'tp'=4] {'req','tp'}, dimensions={0} | all-to-all | bytes 1048576 | tf_op jit(solution)/shard_map/all_to_all | solution.py:137
  239.2 2.7 %collective-permute-start.1 = (bf16[64,512]{1,0:T(8,128)(2,1)S(1)}, bf16[64,512]{1,0:T(8,128)(2,1)S(1)}, u32[]{:S(2)}, u32[]{:S(2)}) collective-permute-start(bf16[64,512]{1,0:T(8,128)(2,1)S(1)} %add_convert_fusion), channel_id=1, source_target_pairs={{0,0},{1,4},{2,8},{3,12},{4,1},{5,5},{6,9},{7,13},{8,2},{9,6},{10,... | collective-permute-start | bytes 196616 | tf_op jit(solution)/shard_map/ppermute | solution.py:139
  242.0 5.2 %collective-permute-done.1 = bf16[64,512]{1,0:T(8,128)(2,1)S(1)} collective-permute-done((bf16[64,512]{1,0:T(8,128)(2,1)S(1)}, bf16[64,512]{1,0:T(8,128)(2,1)S(1)}, u32[]{:S(2)}, u32[]{:S(2)}) %collective-permute-start.1) | collective-permute-done | bytes 65568 | tf_op jit(solution)/shard_map/ppermute | solution.py:139
  (77 shorter events, 5.6 us)
Async XLA Ops:
  6.5 42.9 %copy-start = (bf16[512,512]{1,0:T(8,128)(2,1)S(1)}, bf16[512,512]{1,0:T(8,128)(2,1)}, u32[]{:S(2)}) copy-start(bf16[512,512]{1,0:T(8,128)(2,1)} %param.21) | copy-start | bytes 1572868
  16.0 4.8 %copy-start.12 = (bf16[1,2048,1,128]{3,1,2,0:T(8,128)(2,1)S(1)}, bf16[1,2048,1,128]{3,1,2,0:T(8,128)(2,1)}, u32[]{:S(2)}) copy-start(bf16[1,2048,1,128]{3,1,2,0:T(8,128)(2,1)} %param.18) | copy-start | bytes 1572868
  16.0 4.8 %copy-start.13 = (bf16[256,1,128]{2,0,1:T(8,128)(2,1)S(1)}, bf16[256,1,128]{2,0,1:T(8,128)(2,1)}, u32[]{:S(2)}) copy-start(bf16[256,1,128]{2,0,1:T(8,128)(2,1)} %param.16) | copy-start | bytes 196612
  20.8 8.6 %copy-start.14 = (bf16[64,512]{1,0:T(8,128)(2,1)S(1)}, bf16[64,512]{1,0:T(8,128)(2,1)}, u32[]{:S(2)}) copy-start(bf16[64,512]{1,0:T(8,128)(2,1)} %param.20) | copy-start | bytes 196612
  20.8 13.0 %copy-start.10 = (s32[64,6]{0,1:T(8,128)S(1)}, s32[64,6]{0,1:T(8,128)}, u32[]{:S(2)}) copy-start(s32[64,6]{0,1:T(8,128)} %param.23) | copy-start | bytes 4612
  20.8 13.1 %copy-start.11 = (f32[64,6]{0,1:T(8,128)S(1)}, f32[64,6]{0,1:T(8,128)}, u32[]{:S(2)}) copy-start(f32[64,6]{0,1:T(8,128)} %param.24) | copy-start | bytes 4612
  25.9 17.2 %all-to-all-start = ((f32[4,136,256]{2,1,0:T(8,128)}), f32[4,136,256]{2,1,0:T(8,128)S(1)}, u32[]{:S(2)}, u32[]{:S(2)}) async-start(f32[4,136,256]{2,1,0:T(8,128)} %maximum_bitcast_fusion), calls=%async_computation | async-start | bytes 1114112 | tf_op jit(solution)/shard_map/all_to_all | solution.py:104
  29.4 41.3 %collective-permute-start = (bf16[64,512]{1,0:T(8,128)(2,1)S(1)}, bf16[64,512]{1,0:T(8,128)(2,1)S(1)}, u32[]{:S(2)}, u32[]{:S(2)}) collective-permute-start(bf16[64,512]{1,0:T(8,128)(2,1)S(1)} %copy-done.14), channel_id=1, source_target_pairs={{0,0},{1,4},{2,8},{3,12},{4,1},{5,5},{6,9},{7,13},{8,2},{9,6},{10,... | collective-permute-start | bytes 196616 | tf_op jit(solution)/shard_map/ppermute | solution.py:102
  50.5 20.1 %all-to-all-start.1 = ((f32[4,64,512]{2,1,0:T(8,128)}), f32[4,64,512]{2,1,0:T(8,128)S(1)}, u32[]{:S(2)}, u32[]{:S(2)}) async-start(f32[4,64,512]{2,1,0:T(8,128)} %bitcast.13), calls=%async_computation.1 | async-start | bytes 1048576 | tf_op jit(solution)/shard_map/all_to_all | solution.py:109
  56.2 0.6 copy-start.2
  57.4 55.8 %copy-start.4 = (s32[512,32]{0,1:T(8,128)}, s32[512,32]{0,1:T(8,128)S(1)}, u32[]{:S(2)}) copy-start(s32[512,32]{0,1:T(8,128)S(1)} %reshape.144) | copy-start | bytes 196612
  70.7 42.5 %copy-start.7 = (bf16[64,512]{1,0:T(8,128)(2,1)}, bf16[64,512]{1,0:T(8,128)(2,1)S(1)}, u32[]{:S(2)}) copy-start(bf16[64,512]{1,0:T(8,128)(2,1)S(1)} %collective-permute-done) | copy-start | bytes 196612
  129.2 5.4 %copy-start.3 = (s32[8,64,6]{1,2,0:T(8,128)S(1)}, s32[8,64,6]{1,2,0:T(8,128)}, u32[]{:S(2)}) copy-start(s32[8,64,6]{1,2,0:T(8,128)} %copy-done.2) | copy-start | bytes 36868
  129.2 5.4 %copy-start.9 = (f32[8,64,6]{1,2,0:T(8,128)S(1)}, f32[8,64,6]{1,2,0:T(8,128)}, u32[]{:S(2)}) copy-start(f32[8,64,6]{1,2,0:T(8,128)} %get-tuple-element.13) | copy-start | bytes 36868
  129.3 5.7 %copy-start.15 = (u32[32]{0:T(128)S(1)}, u32[32]{0:T(128)}, u32[]{:S(2)}) copy-start(u32[32]{0:T(128)} %constant.96) | copy-start | bytes 388
  129.3 59.5 %copy-start.5 = (s32[512,32]{0,1:T(8,128)S(1)}, s32[512,32]{0,1:T(8,128)}, u32[]{:S(2)}) copy-start(s32[512,32]{0,1:T(8,128)} %copy-done.4) | copy-start | bytes 196612
  129.3 61.1 %all-to-all-start.2 = ((bf16[4,512,2,352]{1,3,2,0:T(8,128)(2,1)}), bf16[4,512,2,352]{1,3,2,0:T(8,128)(2,1)S(1)}, u32[]{:S(2)}, u32[]{:S(2)}) async-start(bf16[4,512,2,352]{1,3,2,0:T(8,128)(2,1)} %pad_maximum_fusion), calls=%async_computation.2 | async-start | bytes 5767168 | tf_op jit(solution)/shard_map/all_to_all | solution.py:127
  134.6 74.9 %all-gather.4.cloned.1.call-start = ((), (), s32[]{:S(2)}) async-start(), calls=%async_computation.4 | async-start | bytes 1966080 | tf_op jit(solution)/shard_map/all_gather | solution.py:132
  190.8 18.7 %copy-start.6 = (s32[512,32]{0,1:T(8,128)S(1)}, s32[512,32]{0,1:T(8,128)}, u32[]{:S(2)}) copy-start(s32[512,32]{0,1:T(8,128)} %copy-done.4) | copy-start | bytes 196612
  209.5 29.7 %copy-start.8 = (bf16[64,512]{1,0:T(8,128)(2,1)S(1)}, bf16[64,512]{1,0:T(8,128)(2,1)}, u32[]{:S(2)}) copy-start(bf16[64,512]{1,0:T(8,128)(2,1)} %copy-done.7) | copy-start | bytes 196612
  209.5 38.4 %copy-start.1 = (bf16[512,512]{1,0:T(8,128)(2,1)S(1)}, bf16[512,512]{1,0:T(8,128)(2,1)}, u32[]{:S(2)}) copy-start(bf16[512,512]{1,0:T(8,128)(2,1)} %param.21) | copy-start | bytes 1572868
  239.2 8.0 %collective-permute-start.1 = (bf16[64,512]{1,0:T(8,128)(2,1)S(1)}, bf16[64,512]{1,0:T(8,128)(2,1)S(1)}, u32[]{:S(2)}, u32[]{:S(2)}) collective-permute-start(bf16[64,512]{1,0:T(8,128)(2,1)S(1)} %add_convert_fusion), channel_id=1, source_target_pairs={{0,0},{1,4},{2,8},{3,12},{4,1},{5,5},{6,9},{7,13},{8,2},{9,6},{10,... | collective-permute-start | bytes 196616 | tf_op jit(solution)/shard_map/ppermute | solution.py:139
Sparse Core Ops, SparseCore 0:
  192.7 16.7 all-gather.3
where the time goes:
time: 256 us; the launch traced here: 255 us
  blocking collectives  121 us (47%)
  matrix products  38.5 us (15%)
  waiting for transfers between devices  34.6 us (14%)
  starting transfers between devices  21.2 us (8%)
  between operations  14.5 us (6%)
  other arithmetic  14 us (5%)
  local copies, waits for them, and re-layouts  10.6 us (4%)
    psum x1, blocking collectives, body(): squares = lax.psum(squares, 'ctx')  33.5 us
    all_gather x1, blocking collectives, body(): scaled = lax.all_gather(scaled, ('req', 'tp'), tiled=True)  32.5 us
    all_to_all x1, blocking collectives, body(): mixed = lax.all_to_all(mixed, ('req', 'tp'), 0, 0, tiled=True)  21.4 us
    unnamed x1, blocking collectives  18.9 us
    all_gather x1, waiting for transfers between devices, body(): inner = lax.all_gather(inner, 'ctx', tiled=True).reshape(exp_dev, slots, -1)  17 us
    all_to_all x1, waiting for transfers between devices, body(): part = lax.all_to_all(part, 'tp', 0, 0, tiled=True)  12.4 us
    all_gather x1, blocking collectives, route_tables(): both = lax.all_gather(both, ('req', 'ctx'))  9.25 us
    dot_general x1, matrix products, body(): jnp.einsum('esd,edf->esf', rows, w_up, preferred_element_type=jnp.float32)  8.61 us
  transfers between devices with their start and end apart: 6, of which 3 were waited for; matrix products, arithmetic and copies ran while one was open for 2% of the time, Pallas kernels for 0%

commit v1 on v0

--- a/solution.py
+++ b/solution.py
@@ -6,6 +6,16 @@
 TOP = 6
 CAP = 8
 MASKED = -1e30
+
+
+def around_the_ring(array, axis, dim):
+    size = lax.axis_size(axis)
+    held, tiles = (array, [array])
+    for _ in range(size - 1):
+        held = lax.ppermute(held, axis, [(i, (i + 1) % size) for i in range(size)])
+        tiles.insert(0, held)
+    row_of_blocks = jnp.concatenate(tiles, axis=dim)
+    return jnp.roll(row_of_blocks, (lax.axis_index(axis) + 1) * array.shape[dim], axis=dim)
 
 
 def attention_part(queries, new_keys, new_values, cache_keys, cache_values, length):
@@ -103,7 +113,7 @@
     packs = attention_part(queries, new_keys, new_values, cache_keys, cache_values, length)
     packs = lax.all_to_all(packs, "ctx", 0, 0, tiled=True)
     attended = merge(packs, hd, heads)
-    attended = lax.all_gather(attended, "ctx", tiled=True)
+    attended = around_the_ring(attended, "ctx", 0)
     part = jnp.dot(attended, out_weight, preferred_element_type=jnp.float32)
     part = part.reshape(-1, block, share)
     part = lax.all_to_all(part, "tp", 0, 0, tiled=True)

time: 256 us -> 259 us (1.012)
  blocking collectives: 121 us -> 126 us
  starting transfers between devices: 21.2 us -> 18.4 us
    all_to_all x0 -> x1, blocking collectives: none -> 10.6 us  [body(): packs = lax.all_to_all(packs, 'ctx', 0, 0, tiled=True)]
    all_gather x1 -> x0, blocking collectives: 5.85 us -> none  [body(): attended = lax.all_gather(attended, 'ctx', tiled=True)]
    all_to_all x1 -> x0, starting transfers between devices: 3.46 us -> none  [body(): packs = lax.all_to_all(packs, 'ctx', 0, 0, tiled=True)]
    ppermute x0 -> x3, waiting for transfers between devices: none -> 3.32 us  [around_the_ring(): held = lax.ppermute(held, axis, [(i, (i + 1) % size) for i in range(size)])]
  transfers between devices with their start and end apart: 6 -> 8, of which waited for: 3 -> 4; matrix products, arithmetic and copies ran while one was open for 2% -> 2% of each run, Pallas kernels for 0% -> 0%
where the time goes in v1:
time: 259 us; the launch traced here: 258 us
  blocking collectives  126 us (49%)
  matrix products  38.5 us (15%)
  waiting for transfers between devices  36.3 us (14%)
  starting transfers between devices  18.4 us (7%)
  between operations  14.6 us (6%)
  other arithmetic  13.4 us (5%)
  local copies, waits for them, and re-layouts  10.7 us (4%)
    psum x1, blocking collectives, body(): squares = lax.psum(squares, 'ctx')  33.5 us
    all_gather x1, blocking collectives, body(): scaled = lax.all_gather(scaled, ('req', 'tp'), tiled=True)  32.6 us
    all_to_all x1, blocking collectives, body(): mixed = lax.all_to_all(mixed, ('req', 'tp'), 0, 0, tiled=True)  21.4 us
    unnamed x1, blocking collectives  19.1 us
    all_gather x1, waiting for transfers between devices, body(): inner = lax.all_gather(inner, 'ctx', tiled=True).reshape(exp_dev, slots, -1)  17.1 us
    all_to_all x1, blocking collectives, body(): packs = lax.all_to_all(packs, 'ctx', 0, 0, tiled=True)  10.6 us
    all_to_all x1, waiting for transfers between devices, body(): part = lax.all_to_all(part, 'tp', 0, 0, tiled=True)  10.6 us
    all_gather x1, blocking collectives, route_tables(): both = lax.all_gather(both, ('req', 'ctx'))  9.21 us
  transfers between devices with their start and end apart: 8, of which 4 were waited for; matrix products, arithmetic and copies ran while one was open for 2% of the time, Pallas kernels for 0%

profile of v1, /device:TPU:4, one launch (start us, length us, event | category | flops | bytes accessed | tf_op | source)
XLA Modules:
  0.0 258.4 jit_solution(1240053992585343936)
XLA Ops:
  6.6 1.0 copy.55
  7.6 1.2 dynamic_slice.14
  8.9 0.7 add_compare_fusion
  9.5 6.5 %fusion = (f32[1024]{0:T(1024)S(1)}, f32[2304,1024]{1,0:T(8,128)S(1)}) fusion(s32[1024]{0:T(1024)S(1)} %fusion.40, s32[2304]{0:T(1024)S(1)} %iota_add_fusion, pred[2304]{0:T(1024)(128)(4,1)S(1)} %get-tuple-element.17, pred[2304]{0:T(1024)(128)(4,1)S(1)} %get-tuple-element.18, pred[]{:T(512)S(6)} %eq.34, bf16[1024,128]{1,0:T(8,128)(2,1)S(1)} %bitcast.90, ...), kind=kOutput, calls=%fused_computation.3 | convolution fusion | flops 619314176 | bytes 10311169 | tf_op jit(solution)/shard_map/dot_general | solution.py:31
  16.0 4.7 %fusion.1 = f32[1024]{0:T(1024)S(1)} fusion(f32[2304,1024]{1,0:T(8,128)S(1)} %get-tuple-element.16, f32[1024]{0:T(1024)S(1)} %get-tuple-element.15, s32[1024]{0:T(1024)S(1)} %fusion.40, s32[2304]{0:T(1024)S(1)} %iota_add_fusion, pred[2304]{0:T(1024)(128)(4,1)S(1)} %get-tuple-element.17, pred[2304]{0:T(1024)(128)(4,1)S(1)} %get-tuple-element.18, pred[]{:T(512)S(6)} %eq.34), kind=kLoop, calls=%fused_computation.5 | loop fusion | flops 18873344 | bytes 9463297 | tf_op jit(solution)/shard_map/reduce_sum | solution.py:43
  20.8 4.0 %fusion.3 = f32[128,1024]{1,0:T(8,128)S(1)} fusion(f32[2304,1024]{1,0:T(8,128)S(1)} %get-tuple-element.16, f32[1024]{0:T(1024)S(1)} %get-tuple-element.15, s32[1024]{0:T(1024)S(1)} %fusion.40, s32[2304]{0:T(1024)S(1)} %iota_add_fusion, pred[2304]{0:T(1024)(128)(4,1)S(1)} %get-tuple-element.17, pred[2304]{0:T(1024)(128)(4,1)S(1)} %get-tuple-element.18, ...), kind=kOutput, calls=%fused_computation.7 | convolution fusion | flops 624033792 | bytes 10573313 | tf_op jit(solution)/shard_map/dot_general | solution.py:44
  25.1 10.6 %all_to_all.20 = f32[4,136,256]{2,1,0:T(8,128)S(1)} all-to-all(f32[4,136,256]{2,1,0:T(8,128)S(1)} %maximum_bitcast_fusion), channel_id=1, replica_groups=mesh['req'=2,'ctx'=4,'tp'=4] {'ctx'}, dimensions={0} | all-to-all | bytes 1114112 | tf_op jit(solution)/shard_map/all_to_all | solution.py:114
  36.2 5.6 %collective-permute-start.3 = (bf16[64,512]{1,0:T(8,128)(2,1)S(1)}, bf16[64,512]{1,0:T(8,128)(2,1)S(1)}, u32[]{:S(2)}, u32[]{:S(2)}) collective-permute-start(bf16[64,512]{1,0:T(8,128)(2,1)S(1)} %copy-done.14), channel_id=1, source_target_pairs={{0,0},{1,4},{2,8},{3,12},{4,1},{5,5},{6,9},{7,13},{8,2},{9,6},{10,... | collective-permute-start | bytes 196616 | tf_op jit(solution)/shard_map/ppermute | solution.py:112
  41.9 1.2 collective-permute-start.1
  43.1 9.2 %all-gather.1 = f32[8,64,12]{1,2,0:T(8,128)S(1)} all-gather(f32[1,64,12]{1,2,0:T(8,128)S(1)} %maximum_bitcast_fusion.1), channel_id=2, replica_groups=mesh['req'=2,'ctx'=4,'tp'=4] {'req','ctx'}, dimensions={0}, use_global_device_ids=true | all-gather | bytes 27648 | tf_op jit(solution)/shard_map/all_gather | solution.py:66
  52.7 3.3 %collective-permute-done.2 = bf16[64,512]{1,0:T(8,128)(2,1)S(1)} collective-permute-done((bf16[64,512]{1,0:T(8,128)(2,1)S(1)}, bf16[64,512]{1,0:T(8,128)(2,1)S(1)}, u32[]{:S(2)}, u32[]{:S(2)}) %collective-permute-start.2) | collective-permute-done | bytes 65568 | tf_op jit(solution)/shard_map/ppermute | solution.py:15
  56.3 1.1 fusion.26
  57.4 3.5 %all-to-all-start.1 = ((f32[4,64,512]{2,1,0:T(8,128)}), f32[4,64,512]{2,1,0:T(8,128)S(1)}, u32[]{:S(2)}, u32[]{:S(2)}) async-start(f32[4,64,512]{2,1,0:T(8,128)} %bitcast.13), calls=%async_computation.1 | async-start | bytes 1048576 | tf_op jit(solution)/shard_map/all_to_all | solution.py:119
  62.7 0.8 dynamic_slice.16
  63.5 10.6 %all-to-all-done.1 = f32[4,64,512]{2,1,0:T(8,128)S(1)} async-done(((f32[4,64,512]{2,1,0:T(8,128)}), f32[4,64,512]{2,1,0:T(8,128)S(1)}, u32[]{:S(2)}, u32[]{:S(2)}) %all-to-all-start.1) | async-done | bytes 524320 | tf_op jit(solution)/shard_map/all_to_all | solution.py:119
  74.2 32.6 %all_gather.17 = bf16[512,512]{1,0:T(8,128)(2,1)S(1)} all-gather(bf16[64,512]{1,0:T(8,128)(2,1)S(1)} %get-tuple-element.12), channel_id=1, replica_groups=mesh['req'=2,'ctx'=4,'tp'=4] {'req','tp'}, dimensions={0}, use_global_device_ids=true | all-gather | bytes 589824 | tf_op jit(solution)/shard_map/all_gather | solution.py:127
  106.9 1.3 fusion.6
  108.1 8.6 %convolution_convert_fusion = bf16[32,64,352]{2,1,0:T(8,128)(2,1)} fusion(bf16[32,64,512]{2,1,0:T(8,128)(2,1)S(1)} %fusion.6, bf16[32,512,352]{1,2,0:T(8,128)(2,1)} %param.26), kind=kOutput, calls=%fused_computation.17 | convolution fusion | flops 738918400 | bytes 15073280 | tf_op jit(solution)/shard_map/esd,edf->esf/dot_general | solution.py:134
  116.7 2.5 copy.63
  119.3 8.6 %convolution_convert_fusion.1 = bf16[32,64,352]{2,1,0:T(8,128)(2,1)} fusion(bf16[32,64,512]{2,1,0:T(8,128)(2,1)S(1)} %fusion.6, bf16[32,512,352]{1,2,0:T(8,128)(2,1)} %param.25), kind=kOutput, calls=%fused_computation.18 | convolution fusion | flops 738918400 | bytes 15073280 | tf_op jit(solution)/shard_map/esd,edf->esf/dot_general | solution.py:133
  127.9 1.7 copy.62
  129.6 3.2 %pad_maximum_fusion = bf16[4,512,2,352]{1,3,2,0:T(8,128)(2,1)} fusion(bf16[4,512,1,352]{1,3,2,0:T(8,128)(2,1)} %copy.63, bf16[4,512,1,352]{1,3,2,0:T(8,128)(2,1)S(1)} %copy.62), kind=kLoop, calls=%fused_computation.14 | loop fusion | flops 1441792 | bytes 5767168 | tf_op jit(solution)/shard_map/stack | solution.py:135
  132.8 5.0 %all-to-all-start.2 = ((bf16[4,512,2,352]{1,3,2,0:T(8,128)(2,1)}), bf16[4,512,2,352]{1,3,2,0:T(8,128)(2,1)S(1)}, u32[]{:S(2)}, u32[]{:S(2)}) async-start(bf16[4,512,2,352]{1,3,2,0:T(8,128)(2,1)} %pad_maximum_fusion), calls=%async_computation.2 | async-start | bytes 5767168 | tf_op jit(solution)/shard_map/all_to_all | solution.py:137
  139.5 33.5 %psum.7 = f32[64]{0:T(128)S(1)} all-reduce(f32[64]{0:T(128)S(1)} %get-tuple-element.11), channel_id=1, replica_groups=mesh['req'=2,'ctx'=4,'tp'=4] {'ctx'}, use_global_device_ids=true, to_apply=%region_9.10 | all-reduce | flops 64 | bytes 512 | tf_op jit(solution)/shard_map/psum | solution.py:124
  173.1 19.1 %all-reduce = f32[512]{0:T(512)S(1)} all-reduce(f32[512]{0:T(512)S(1)} %rsqrt_dynamic-update-slice_fusion), channel_id=1, replica_groups=mesh['req'=2,'ctx'=4,'tp'=4] {'req','tp'}, use_global_device_ids=true, to_apply=%add | all-reduce | flops 512 | bytes 4096
  192.3 1.5 select_reduce_fusion
  195.0 1.0 fusion.16
  196.0 17.1 %all-gather.4.cloned.1.call-done = bf16[2048,352]{1,0:T(8,128)(2,1)} async-done(((bf16[512,352]{1,0:T(8,128)(2,1)}), bf16[2048,352]{1,0:T(8,128)(2,1)}) %all-gather.4.cloned.1.call-update) | async-done | bytes 1441808 | tf_op jit(solution)/shard_map/all_gather | solution.py:142
  213.2 8.2 %fusion.10 = bf16[512,512]{1,0:T(8,128)(2,1)S(1)} fusion(s32[32,512]{1,0:T(8,128)S(1)} %bitcast.93, bf16[32,64,352]{2,1,0:T(8,128)(2,1)} %bitcast.99, bf16[32,352,512]{2,1,0:T(8,128)(2,1)} %param.27, f32[32,64]{1,0:T(8,128)S(1)} %get-tuple-element.5), kind=kOutput, calls=%fused_computation.20 | convolution fusion | flops 1815347200 | bytes 13574144 | tf_op jit(solution)/shard_map/est,esd->td/dot_general | solution.py:145
  221.4 21.4 %all_to_all.21 = bf16[8,64,512]{2,1,0:T(8,128)(2,1)S(1)} all-to-all(bf16[8,64,512]{2,1,0:T(8,128)(2,1)S(1)} %bitcast.89), channel_id=1, replica_groups=mesh['req'=2,'ctx'=4,'tp'=4] {'req','tp'}, dimensions={0} | all-to-all | bytes 1048576 | tf_op jit(solution)/shard_map/all_to_all | solution.py:147
  242.9 2.7 %collective-permute-start.4 = (bf16[64,512]{1,0:T(8,128)(2,1)S(1)}, bf16[64,512]{1,0:T(8,128)(2,1)S(1)}, u32[]{:S(2)}, u32[]{:S(2)}) collective-permute-start(bf16[64,512]{1,0:T(8,128)(2,1)S(1)} %add_convert_fusion), channel_id=1, source_target_pairs={{0,0},{1,4},{2,8},{3,12},{4,1},{5,5},{6,9},{7,13},{8,2},{9,6},{10,... | collective-permute-start | bytes 196616 | tf_op jit(solution)/shard_map/ppermute | solution.py:149
  245.6 5.3 %collective-permute-done.4 = bf16[64,512]{1,0:T(8,128)(2,1)S(1)} collective-permute-done((bf16[64,512]{1,0:T(8,128)(2,1)S(1)}, bf16[64,512]{1,0:T(8,128)(2,1)S(1)}, u32[]{:S(2)}, u32[]{:S(2)}) %collective-permute-start.4) | collective-permute-done | bytes 65568 | tf_op jit(solution)/shard_map/ppermute | solution.py:149
  (89 shorter events, 6.4 us)
Async XLA Ops:
  6.5 49.7 %copy-start = (bf16[512,512]{1,0:T(8,128)(2,1)S(1)}, bf16[512,512]{1,0:T(8,128)(2,1)}, u32[]{:S(2)}) copy-start(bf16[512,512]{1,0:T(8,128)(2,1)} %param.21) | copy-start | bytes 1572868
  16.0 4.8 %copy-start.12 = (bf16[1,2048,1,128]{3,1,2,0:T(8,128)(2,1)S(1)}, bf16[1,2048,1,128]{3,1,2,0:T(8,128)(2,1)}, u32[]{:S(2)}) copy-start(bf16[1,2048,1,128]{3,1,2,0:T(8,128)(2,1)} %param.18) | copy-start | bytes 1572868
  16.0 4.8 %copy-start.13 = (bf16[256,1,128]{2,0,1:T(8,128)(2,1)S(1)}, bf16[256,1,128]{2,0,1:T(8,128)(2,1)}, u32[]{:S(2)}) copy-start(bf16[256,1,128]{2,0,1:T(8,128)(2,1)} %param.16) | copy-start | bytes 196612
  24.8 11.4 %copy-start.14 = (bf16[64,512]{1,0:T(8,128)(2,1)S(1)}, bf16[64,512]{1,0:T(8,128)(2,1)}, u32[]{:S(2)}) copy-start(bf16[64,512]{1,0:T(8,128)(2,1)} %param.20) | copy-start | bytes 196612
  24.8 17.0 %copy-start.10 = (s32[64,6]{0,1:T(8,128)S(1)}, s32[64,6]{0,1:T(8,128)}, u32[]{:S(2)}) copy-start(s32[64,6]{0,1:T(8,128)} %param.23) | copy-start | bytes 4612
  24.8 18.2 %copy-start.11 = (f32[64,6]{0,1:T(8,128)S(1)}, f32[64,6]{0,1:T(8,128)}, u32[]{:S(2)}) copy-start(f32[64,6]{0,1:T(8,128)} %param.24) | copy-start | bytes 4612
  36.1 5.7 %collective-permute-start = (bf16[64,512]{1,0:T(8,128)(2,1)S(1)}, bf16[64,512]{1,0:T(8,128)(2,1)S(1)}, u32[]{:S(2)}, u32[]{:S(2)}) collective-permute-start(bf16[64,512]{1,0:T(8,128)(2,1)S(1)} %copy_bitcast_fusion.1), channel_id=1, source_target_pairs={{0,4},{4,8},{8,12},{12,0},{1,5},{5,9},{9,13},{13,1},{2,6},{6,10},{... | collective-permute-start | bytes 196616 | tf_op jit(solution)/shard_map/ppermute | solution.py:15
  36.2 37.9 %collective-permute-start.3 = (bf16[64,512]{1,0:T(8,128)(2,1)S(1)}, bf16[64,512]{1,0:T(8,128)(2,1)S(1)}, u32[]{:S(2)}, u32[]{:S(2)}) collective-permute-start(bf16[64,512]{1,0:T(8,128)(2,1)S(1)} %copy-done.14), channel_id=1, source_target_pairs={{0,0},{1,4},{2,8},{3,12},{4,1},{5,5},{6,9},{7,13},{8,2},{9,6},{10,... | collective-permute-start | bytes 196616 | tf_op jit(solution)/shard_map/ppermute | solution.py:112
  41.9 10.4 %collective-permute-start.1 = (bf16[64,512]{1,0:T(8,128)(2,1)S(1)}, bf16[64,512]{1,0:T(8,128)(2,1)S(1)}, u32[]{:S(2)}, u32[]{:S(2)}) collective-permute-start(bf16[64,512]{1,0:T(8,128)(2,1)S(1)} %collective-permute-done), channel_id=1, source_target_pairs={{0,4},{4,8},{8,12},{12,0},{1,5},{5,9},{9,13},{13,1},{2,6},{6,10},{... | collective-permute-start | bytes 196616 | tf_op jit(solution)/shard_map/ppermute | solution.py:15
  52.3 3.7 %collective-permute-start.2 = (bf16[64,512]{1,0:T(8,128)(2,1)S(1)}, bf16[64,512]{1,0:T(8,128)(2,1)S(1)}, u32[]{:S(2)}, u32[]{:S(2)}) collective-permute-start(bf16[64,512]{1,0:T(8,128)(2,1)S(1)} %collective-permute-done.1), channel_id=1, source_target_pairs={{0,4},{4,8},{8,12},{12,0},{1,5},{5,9},{9,13},{13,1},{2,6},{6,10},{... | collective-permute-start | bytes 196616 | tf_op jit(solution)/shard_map/ppermute | solution.py:15
  57.4 16.7 %all-to-all-start.1 = ((f32[4,64,512]{2,1,0:T(8,128)}), f32[4,64,512]{2,1,0:T(8,128)S(1)}, u32[]{:S(2)}, u32[]{:S(2)}) async-start(f32[4,64,512]{2,1,0:T(8,128)} %bitcast.13), calls=%async_computation.1 | async-start | bytes 1048576 | tf_op jit(solution)/shard_map/all_to_all | solution.py:119
  61.5 0.6 copy-start.2
  62.7 54.1 %copy-start.4 = (s32[512,32]{0,1:T(8,128)}, s32[512,32]{0,1:T(8,128)S(1)}, u32[]{:S(2)}) copy-start(s32[512,32]{0,1:T(8,128)S(1)} %reshape.144) | copy-start | bytes 196612
  74.1 42.6 %copy-start.7 = (bf16[64,512]{1,0:T(8,128)(2,1)}, bf16[64,512]{1,0:T(8,128)(2,1)S(1)}, u32[]{:S(2)}) copy-start(bf16[64,512]{1,0:T(8,128)(2,1)S(1)} %collective-permute-done.3) | copy-start | bytes 196612
  132.8 5.0 %copy-start.3 = (s32[8,64,6]{1,2,0:T(8,128)S(1)}, s32[8,64,6]{1,2,0:T(8,128)}, u32[]{:S(2)}) copy-start(s32[8,64,6]{1,2,0:T(8,128)} %copy-done.2) | copy-start | bytes 36868
  132.8 5.0 %copy-start.9 = (f32[8,64,6]{1,2,0:T(8,128)S(1)}, f32[8,64,6]{1,2,0:T(8,128)}, u32[]{:S(2)}) copy-start(f32[8,64,6]{1,2,0:T(8,128)} %get-tuple-element.13) | copy-start | bytes 36868
  132.8 5.4 %copy-start.15 = (u32[32]{0:T(128)S(1)}, u32[32]{0:T(128)}, u32[]{:S(2)}) copy-start(u32[32]{0:T(128)} %constant.117) | copy-start | bytes 388
  132.8 59.4 %copy-start.5 = (s32[512,32]{0,1:T(8,128)S(1)}, s32[512,32]{0,1:T(8,128)}, u32[]{:S(2)}) copy-start(s32[512,32]{0,1:T(8,128)} %copy-done.4) | copy-start | bytes 196612
  132.8 61.0 %all-to-all-start.2 = ((bf16[4,512,2,352]{1,3,2,0:T(8,128)(2,1)}), bf16[4,512,2,352]{1,3,2,0:T(8,128)(2,1)S(1)}, u32[]{:S(2)}, u32[]{:S(2)}) async-start(bf16[4,512,2,352]{1,3,2,0:T(8,128)(2,1)} %pad_maximum_fusion), calls=%async_computation.2 | async-start | bytes 5767168 | tf_op jit(solution)/shard_map/all_to_all | solution.py:137
  137.8 75.3 %all-gather.4.cloned.1.call-start = ((), (), s32[]{:S(2)}) async-start(), calls=%async_computation.4 | async-start | bytes 1966080 | tf_op jit(solution)/shard_map/all_gather | solution.py:142
  194.3 18.8 %copy-start.6 = (s32[512,32]{0,1:T(8,128)S(1)}, s32[512,32]{0,1:T(8,128)}, u32[]{:S(2)}) copy-start(s32[512,32]{0,1:T(8,128)} %copy-done.4) | copy-start | bytes 196612
  213.1 29.7 %copy-start.8 = (bf16[64,512]{1,0:T(8,128)(2,1)S(1)}, bf16[64,512]{1,0:T(8,128)(2,1)}, u32[]{:S(2)}) copy-start(bf16[64,512]{1,0:T(8,128)(2,1)} %copy-done.7) | copy-start | bytes 196612
  213.1 38.4 %copy-start.1 = (bf16[512,512]{1,0:T(8,128)(2,1)S(1)}, bf16[512,512]{1,0:T(8,128)(2,1)}, u32[]{:S(2)}) copy-start(bf16[512,512]{1,0:T(8,128)(2,1)} %param.21) | copy-start | bytes 1572868
  242.9 8.0 %collective-permute-start.4 = (bf16[64,512]{1,0:T(8,128)(2,1)S(1)}, bf16[64,512]{1,0:T(8,128)(2,1)S(1)}, u32[]{:S(2)}, u32[]{:S(2)}) collective-permute-start(bf16[64,512]{1,0:T(8,128)(2,1)S(1)} %add_convert_fusion), channel_id=1, source_target_pairs={{0,0},{1,4},{2,8},{3,12},{4,1},{5,5},{6,9},{7,13},{8,2},{9,6},{10,... | collective-permute-start | bytes 196616 | tf_op jit(solution)/shard_map/ppermute | solution.py:149
Sparse Core Ops, SparseCore 0:
  196.2 16.9 all-gather.3
